TPU v7x, 32 devices: a whole 2x2x4 slice. The times are simulated.
32 devices in a mesh: ids: 8 (over z, x), mdl: 4 (over y, core).
Axes of the slice: x: 2, y: 2, z: 4, core: 2. Of those that a mesh axis runs over, the one named last changes fastest.
Arguments:
- hash_codes: int32 [32768, 1024], P('ids', 'mdl'), may hold values from 0 to 1023
- request_ids: int32 [64, 1024], P('ids'), may hold values from 0 to 32767, as said below
- request_counts: int32 [64], P('ids'), may hold values from 256 to 1024, as said below
- token_slots: int32 [65536], P('ids'), may hold values from 0 to 8191, as said below
- cotangent: bfloat16 [65536, 32], P('ids'), may hold values from -6 to 6
- weight_first: float32 [1024, 1800], P('ids', 'mdl'), may hold values from -0.1875 to 0.1875
- weight_second: float32 [1800, 1800], P(None, 'mdl'), may hold values from -0.125 to 0.125
- weight_final: float32 [1800, 32], P('mdl'), may hold values from -0.125 to 0.125
- norm_params: float32 [4, 1800], P(None, 'mdl')
- bias_final: float32 [32], replicated, may hold values from -0.5 to 0.5
- moment_first: float32 [1024, 1800], P('ids', 'mdl'), may hold values from -0.0007324219 to 0.0007324219
- square_first: float32 [1024, 1800], P('ids', 'mdl'), may hold values from 1.373291e-09 to 5.493164e-09
- moment_second: float32 [1800, 1800], P(None, 'mdl'), may hold values from -0.0007324219 to 0.0007324219
- square_second: float32 [1800, 1800], P(None, 'mdl'), may hold values from 1.373291e-09 to 5.493164e-09
- moment_final: float32 [1800, 32], P('mdl'), may hold values from -0.0048828125 to 0.0048828125
- square_final: float32 [1800, 32], P('mdl'), may hold values from 6.103516e-08 to 2.4414064e-07
- moment_norm: float32 [4, 1800], P(None, 'mdl'), may hold values from -0.001953125 to 0.001953125
- square_norm: float32 [4, 1800], P(None, 'mdl'), may hold values from 9e-09 to 3.6e-08
- moment_bias: float32 [32], replicated, may hold values from -0.03125 to 0.03125
- square_bias: float32 [32], replicated, may hold values from 2.5e-06 to 1e-05
Outputs:
- token_embed: bfloat16 [65536, 32], P('ids')
- momentum_first: float32 [1024, 1800], P('ids', 'mdl')
- variance_first: float32 [1024, 1800], P('ids', 'mdl')
- master_first: float32 [1024, 1800], P('ids', 'mdl')
- bfloat_first: bfloat16 [1024, 1800], P('ids', 'mdl')
- momentum_second: float32 [1800, 1800], P(None, 'mdl')
- variance_second: float32 [1800, 1800], P(None, 'mdl')
- master_second: float32 [1800, 1800], P(None, 'mdl')
- bfloat_second: bfloat16 [1800, 1800], P(None, 'mdl')
- momentum_final: float32 [1800, 32], P('mdl')
- variance_final: float32 [1800, 32], P('mdl')
- master_final: float32 [1800, 32], P('mdl')
- bfloat_final: bfloat16 [1800, 32], P('mdl')
- momentum_norm: float32 [4, 1800], P(None, 'mdl')
- variance_norm: float32 [4, 1800], P(None, 'mdl')
- master_norm: float32 [4, 1800], P(None, 'mdl')
- momentum_bias: float32 [32], replicated
- variance_bias: float32 [32], replicated
- master_bias: float32 [32], replicated
Inputs may be any that keep to these rules, and one draw needn't show every extreme that they name: `request_ids`: entries of row s * 8 + j lie in owner j's range j * 4096 to (j + 1) * 4096 - 1; the live ones (the first request_counts of the row) are distinct; the others are padding. `request_counts`: some owner receives exactly 1024 live ids from every device. `token_slots`: each token points at a live slot of its own device, and every live slot of a device is pointed at by one or more of its tokens.
All inputs are finite; a program needn't handle non-finite values.
Results may differ from a plain program's by a relative error of at most 0.003.
The roundings to bfloat16 on the way count: a program that leaves them out, or rounds other values in their place, can miss the bound.
Values may be sent and summed in bfloat16 or wider, within the bound.
A program may use at most 256 MiB of HBM per device.

v0:
```python
import jax
import jax.numpy as jnp
from jax import lax
from jax.sharding import PartitionSpec as P

STEP = 10
beta_one = 0.9
beta_two = 0.999
adam_epsilon = 1e-08
norm_epsilon = 1e-05
penalty_weight = 0.25
decay_matrix = 0.01
rate_matrix = 0.05
rate_norm = 0.5
rate_bias = 0.02
LANES = 128


def mish_parts(inputs):
    grown = jnp.exp(jnp.minimum(inputs, 20.0))
    above = grown * (grown + 2.0)
    inverse = 1.0 / (above + 2.0)
    return (grown, above * inverse, inverse)


def mish(inputs):
    return inputs * mish_parts(inputs)[1]


def mish_slope(inputs):
    grown, gate, inverse = mish_parts(inputs)
    return gate + 4.0 * jnp.minimum(inputs, 20.0) * (grown * inverse) * ((1.0 + grown) * inverse)


def contract(left, right, left_dim, right_dim):
    return lax.dot_general(
        left, right, (((left_dim,), (right_dim,)), ((), ())), preferred_element_type=jnp.float32
    )


def norm_back(upstream, unit_rows, gain_row, scale_row, live_mask, gain_sum, shift_sum, live_count):
    return scale_row * (
        gain_row * upstream
        - live_mask[:, None] * gain_row * (shift_sum + unit_rows * gain_sum) / live_count
    )


def adam(weight, moment, square, gradient, step_rate, shrink):
    momentum = beta_one * moment + (1.0 - beta_one) * gradient
    variance = beta_two * square + (1.0 - beta_two) * gradient * gradient
    moment_hat = momentum / (1.0 - beta_one**STEP)
    square_hat = variance / (1.0 - beta_two**STEP)
    master = weight - step_rate * (
        moment_hat / (jnp.sqrt(square_hat) + adam_epsilon) + shrink * weight
    )
    return (momentum, variance, master)


def split_two(values):
    high = values.astype(jnp.bfloat16)
    low = (values - high.astype(jnp.float32)).astype(jnp.bfloat16)
    return (high, low)


def one_hot(index, length, first):
    rows = lax.broadcasted_iota(jnp.int32, (length, index.shape[0]), 0) + first
    return (rows == index[None, :]).astype(jnp.bfloat16)


def body(
    hash_codes,
    request_ids,
    request_counts,
    token_slots,
    cotangent,
    weight_first,
    weight_second,
    weight_final,
    norm_params,
    bias_final,
    moment_first,
    square_first,
    moment_second,
    square_second,
    moment_final,
    square_final,
    moment_norm,
    square_norm,
    moment_bias,
    square_bias,
):
    owners = lax.axis_size("ids")
    parts = lax.axis_size("mdl")
    part = lax.axis_index("mdl")
    both = ("ids", "mdl")
    range_rows = hash_codes.shape[0]
    rows = range_rows // parts
    slots_per = request_ids.shape[1]
    piece = slots_per // parts
    out_width = weight_final.shape[1]
    width = weight_first.shape[1]
    wide = width + -width % LANES
    hidden = wide * parts
    more = wide - width
    token_count = token_slots.shape[0]
    token_piece = token_count // parts
    token_total = token_count * owners
    first_part = jnp.pad(weight_first.astype(jnp.bfloat16), ((0, 0), (0, more)))
    first_low = lax.all_gather(first_part, "ids", axis=0, tiled=True)
    first_low = lax.all_gather(first_low, "mdl", axis=1, tiled=True)
    second_part = jnp.pad(
        weight_second.astype(jnp.bfloat16).reshape(parts, width, width),
        ((0, 0), (0, more), (0, more)),
    ).reshape(hidden, wide)
    second_low = lax.all_gather(second_part, "mdl", axis=1, tiled=True)
    final_part = jnp.pad(weight_final.astype(jnp.bfloat16), ((0, more), (0, 0)))
    final_low = lax.all_gather(final_part, "mdl", axis=0, tiled=True)
    norm_all = lax.all_gather(jnp.pad(norm_params, ((0, 0), (0, more))), "mdl", axis=1, tiled=True)
    encoded = ((hash_codes.astype(jnp.float32) + 0.5) / 512.0 - 1.0).astype(jnp.bfloat16)
    features = lax.all_to_all(encoded, "mdl", split_axis=0, concat_axis=1, tiled=True)
    owner_row = jnp.arange(owners, dtype=jnp.int32)[:, None]
    wanted = jnp.where(
        jnp.arange(slots_per, dtype=jnp.int32)[None, :] < request_counts[:, None],
        request_ids - owner_row * range_rows,
        range_rows,
    )
    received = lax.all_to_all(wanted, "ids", split_axis=0, concat_axis=0, tiled=True)
    slot_owner = token_slots // slots_per
    slot_place = token_slots % slots_per - part * piece
    slot_here = jnp.where(
        (slot_place >= 0) & (slot_place < piece), slot_owner * piece + slot_place, -1
    )
    slot_sum = (
        jnp.dot(
            one_hot(slot_here, owners * piece, 0), cotangent, preferred_element_type=jnp.float32
        )
        / token_total
    )
    high, low = split_two(slot_sum)
    sent = jnp.concatenate([high, low], axis=1).reshape(owners, piece * 2 * out_width)
    arrived = lax.all_to_all(sent, "ids", split_axis=0, concat_axis=0, tiled=True)
    arrived = lax.all_gather(
        arrived.reshape(owners * piece, 2 * out_width), "mdl", axis=0, tiled=False
    )
    arrived = arrived.reshape(parts * owners * piece, 2 * out_width)
    slot_rows = received.reshape(owners, parts, piece).transpose(1, 0, 2)
    slot_rows = slot_rows.reshape(-1)
    marked = jnp.concatenate(
        [arrived, jnp.ones((arrived.shape[0], 2 * out_width), jnp.bfloat16)], axis=1
    )
    row_sums = jnp.dot(
        one_hot(slot_rows, rows, part * rows), marked, preferred_element_type=jnp.float32
    )
    row_grad = row_sums[:, :out_width] + row_sums[:, out_width : 2 * out_width]
    live_mask = jnp.minimum(row_sums[:, 2 * out_width], 1.0)
    linear_one = jnp.dot(features, first_low, preferred_element_type=jnp.float32)
    active_one = mish(linear_one)
    weighted_one = live_mask[:, None] * active_one
    sums_one = jnp.stack([jnp.sum(weighted_one, 0), jnp.sum(weighted_one * active_one, 0)])
    sums_one, live_count = lax.psum((sums_one, jnp.sum(live_mask)), both)
    mean_one = sums_one[0] / live_count
    scale_one = lax.rsqrt(sums_one[1] / live_count - mean_one * mean_one + norm_epsilon)
    unit_one = (active_one - mean_one) * scale_one
    normed_one = (norm_all[0] * unit_one + norm_all[1]).astype(jnp.bfloat16)
    linear_two = jnp.dot(normed_one, second_low, preferred_element_type=jnp.float32)
    active_two = mish(linear_two)
    weighted_two = live_mask[:, None] * active_two
    sums_two = lax.psum(
        jnp.stack([jnp.sum(weighted_two, 0), jnp.sum(weighted_two * active_two, 0)]), both
    )
    mean_two = sums_two[0] / live_count
    scale_two = lax.rsqrt(sums_two[1] / live_count - mean_two * mean_two + norm_epsilon)
    unit_two = (active_two - mean_two) * scale_two
    normed_two = (norm_all[2] * unit_two + norm_all[3]).astype(jnp.bfloat16)
    embedding = jnp.dot(normed_two, final_low, preferred_element_type=jnp.float32) + bias_final
    embed_low = embedding.astype(jnp.bfloat16)
    embed_range = lax.all_gather(embed_low, "mdl", axis=0, tiled=True)
    slots_mine = lax.dynamic_slice(received, (0, part * piece), (owners, piece)).reshape(-1)
    pick_rows = (
        slots_mine[:, None] == lax.broadcasted_iota(jnp.int32, (owners * piece, range_rows), 1)
    ).astype(jnp.bfloat16)
    replies = jnp.dot(pick_rows, embed_range, preferred_element_type=jnp.float32)
    replies = replies.astype(jnp.bfloat16).reshape(owners, piece * out_width)
    returned = lax.all_to_all(replies, "ids", split_axis=0, concat_axis=0, tiled=True)
    returned = lax.all_gather(returned.reshape(owners, piece, out_width), "mdl", axis=1, tiled=True)
    returned = returned.reshape(owners * slots_per, out_width)
    tokens_mine = lax.dynamic_slice(token_slots, (part * token_piece,), (token_piece,))
    pick_slots = (
        tokens_mine[:, None]
        == lax.broadcasted_iota(jnp.int32, (token_piece, owners * slots_per), 1)
    ).astype(jnp.bfloat16)
    token_part = jnp.dot(pick_slots, returned, preferred_element_type=jnp.float32)
    token_embed = lax.all_gather(token_part.astype(jnp.bfloat16), "mdl", axis=0, tiled=True)
    grad_embed = (
        row_grad + 2.0 * penalty_weight / live_count * live_mask[:, None] * embedding
    ).astype(jnp.bfloat16)
    incoming_two = contract(grad_embed, final_low, 1, 1)
    sums_two = lax.psum(
        jnp.stack([jnp.sum(incoming_two * unit_two, 0), jnp.sum(incoming_two, 0)]), both
    )
    local_final = contract(normed_two, grad_embed, 0, 0)
    local_bias = jnp.sum(grad_embed.astype(jnp.float32), 0)
    outgoing_two = norm_back(
        incoming_two,
        unit_two,
        norm_all[2],
        scale_two,
        live_mask,
        sums_two[0],
        sums_two[1],
        live_count,
    )
    grad_linear_two = (mish_slope(linear_two) * outgoing_two).astype(jnp.bfloat16)
    local_second = jnp.stack(
        [
            contract(normed_one, grad_linear_two[:, wide * k : wide * (k + 1)], 0, 0)
            for k in range(parts)
        ]
    )
    grad_second = lax.psum_scatter(local_second, "mdl", scatter_dimension=0, tiled=False)
    grad_second = lax.psum(grad_second, "ids")
    grad_second = grad_second.reshape(parts, wide, wide)[:, :width, :width].reshape(-1, width)
    incoming_one = contract(grad_linear_two, second_low, 1, 1)
    sums_one, final_sum, grad_bias = lax.psum(
        (
            jnp.stack([jnp.sum(incoming_one * unit_one, 0), jnp.sum(incoming_one, 0)]),
            local_final,
            local_bias,
        ),
        both,
    )
    outgoing_one = norm_back(
        incoming_one,
        unit_one,
        norm_all[0],
        scale_one,
        live_mask,
        sums_one[0],
        sums_one[1],
        live_count,
    )
    grad_linear_one = (mish_slope(linear_one) * outgoing_one).astype(jnp.bfloat16)
    local_first = jnp.stack(
        [
            contract(features, grad_linear_one[:, wide * k : wide * (k + 1)], 0, 0)
            for k in range(parts)
        ]
    )
    grad_first = lax.psum_scatter(local_first, "mdl", scatter_dimension=0, tiled=False)
    grad_first = lax.psum_scatter(grad_first, "ids", scatter_dimension=0, tiled=True)[:, :width]
    start = part * wide
    grad_final = lax.dynamic_slice(final_sum, (start, 0), (width, out_width))
    grad_norm = lax.dynamic_slice(jnp.concatenate([sums_one, sums_two]), (0, start), (4, width))
    momentum_first, variance_first, master_first = adam(
        weight_first, moment_first, square_first, grad_first, rate_matrix, decay_matrix
    )
    momentum_second, variance_second, master_second = adam(
        weight_second, moment_second, square_second, grad_second, rate_matrix, decay_matrix
    )
    momentum_final, variance_final, master_final = adam(
        weight_final, moment_final, square_final, grad_final, rate_matrix, decay_matrix
    )
    momentum_norm, variance_norm, master_norm = adam(
        norm_params, moment_norm, square_norm, grad_norm, rate_norm, 0.0
    )
    momentum_bias, variance_bias, master_bias = adam(
        bias_final, moment_bias, square_bias, grad_bias, rate_bias, 0.0
    )
    return (
        token_embed,
        momentum_first,
        variance_first,
        master_first,
        master_first.astype(jnp.bfloat16),
        momentum_second,
        variance_second,
        master_second,
        master_second.astype(jnp.bfloat16),
        momentum_final,
        variance_final,
        master_final,
        master_final.astype(jnp.bfloat16),
        momentum_norm,
        variance_norm,
        master_norm,
        momentum_bias,
        variance_bias,
        master_bias,
    )


def solution(mesh):
    rows = P("ids", None)
    grid = P("ids", "mdl")
    columns = P(None, "mdl")
    mdl_rows = P("mdl", None)
    return jax.shard_map(
        body,
        mesh=mesh,
        in_specs=(grid, rows, P("ids"), P("ids"), rows, grid, columns, mdl_rows, columns, P())
        + (grid,) * 2
        + (columns,) * 2
        + (mdl_rows,) * 2
        + (columns,) * 2
        + (P(),) * 2,
        out_specs=(rows,)
        + (grid,) * 4
        + (columns,) * 4
        + (mdl_rows,) * 4
        + (columns,) * 3
        + (P(),) * 3,
        check_vma=False,
    )
```

profile of v0, /device:TPU:0, one launch (start us, length us, event | category | flops | bytes accessed | tf_op | source)
XLA Modules:
  0.0 1000.3 jit_solution(2400045335157976259)
XLA Ops:
  9.8 13.0 %subtract_convert_fusion = (bf16[2048,32]{0,1:T(8,128)(2,1)S(1)}, bf16[2048,32]{0,1:T(8,128)(2,1)S(1)}) fusion(bf16[8192,32]{0,1:T(8,128)(2,1)S(1)} %copy-done, s32[8192]{0:T(1024)S(1)} %fusion.37), kind=kOutput, calls=%fused_computation.68 | convolution fusion | flops 1090846720 | bytes 819200 | tf_op jit(solution)/shard_map/dot_general | solution.py:134
  24.0 2.2 reduce.4
  26.4 18.5 %all_to_all.48 = bf16[8,2,8192]{2,1,0:T(2,128)(2,1)S(1)} all-to-all(bf16[8,2,8192]{2,1,0:T(2,128)(2,1)S(1)} %reshape.107), channel_id=1, replica_groups=mesh['ids'=8,'mdl'=4] {'ids'}, dimensions={0} | all-to-all | bytes 524288 | tf_op jit(solution)/shard_map/all_to_all | solution.py:141
  48.2 5.1 all-gather.5.cloned.1.call-done
  53.7 3.4 convert_element_type.79
  57.1 5.6 reshape.96
  66.3 5.0 all-to-all-start
  71.3 4.1 add_convert_fusion.2
  75.4 2.6 all-to-all-done
  78.0 3.7 all-to-all-start.1
  81.7 48.9 %all_gather.27 = f32[4,2048]{1,0:T(4,128)S(1)} all-gather(f32[4,512]{1,0:T(4,128)S(1)} %pad.17), channel_id=1, replica_groups=mesh['ids'=8,'mdl'=4] {'mdl'}, dimensions={1}, use_global_device_ids=true | all-gather | bytes 40960 | tf_op jit(solution)/shard_map/all_gather | solution.py:118
  130.7 5.4 all_gather.32
  136.2 2.4 copy.86
  140.1 6.3 fusion.4
  147.0 11.5 %multiply_reduce_fusion.1 = (f32[2048]{0:T(1024)S(1)}, f32[2048]{0:T(1024)S(1)}, f32[1024,2048]{1,0:T(8,128)}) fusion(f32[1024]{0:T(1024)S(1)} %bitcast.109, bf16[1024,1024]{0,1:T(8,128)(2,1)S(1)} %bitcast.85, bf16[1024,2048]{0,1:T(8,128)(2,1)} %all-gather.7.cloned.1.call-done), kind=kOutput, calls=%fused_computation.19 | convolution fusion | flops 4318031872 | bytes 14700544 | tf_op jit(solution)/shard_map/dot_general | solution.py:156
  158.5 39.1 %all-reduce.6 = (f32[2,2048]{1,0:T(2,128)S(1)}, f32[]{:T(128)}) all-reduce(f32[2,2048]{1,0:T(2,128)S(1)} %pad_maximum_fusion.3, f32[]{:T(128)} %get-tuple-element.151), channel_id=1, replica_groups=mesh['ids'=8,'mdl'=4] {'ids','mdl'}, use_global_device_ids=true, to_apply=%region_2.3 | all-reduce | flops 4097 | bytes 32776 | tf_op jit(solution)/shard_map/psum | solution.py:160
  198.9 7.3 add_convert_fusion.1
  206.2 18.3 %multiply_reduce_fusion = (f32[2048]{0:T(1024)S(1)}, f32[2048]{0:T(1024)S(1)}, f32[1024,2048]{1,0:T(8,128)}, f32[1024,2048]{1,0:T(8,128)}) fusion(f32[1024]{0:T(1024)S(1)} %bitcast.110, bf16[1024,2048]{1,0:T(8,128)(2,1)} %add_convert_fusion.1, bf16[2048,2048]{0,1:T(8,128)(2,1)} %all-gather.11.cloned.1.call-done), kind=kOutput, calls=%fused_computation.17 | convolution fusion | flops 8612999168 | bytes 29380608 | tf_op jit(solution)/shard_map/dot_general | solution.py:165
  224.5 40.1 %psum.58 = f32[2,2048]{1,0:T(2,128)S(1)} all-reduce(f32[2,2048]{1,0:T(2,128)S(1)} %pad_maximum_fusion.4), channel_id=1, replica_groups=mesh['ids'=8,'mdl'=4] {'ids','mdl'}, use_global_device_ids=true, to_apply=%region_7.8 | all-reduce | flops 4096 | bytes 32768 | tf_op jit(solution)/shard_map/psum | solution.py:168
  265.5 5.1 convert_reduce_fusion
  270.6 4.2 multiply_reduce_fusion.3
  274.9 40.2 %psum.59 = f32[2,2048]{1,0:T(2,128)S(1)} all-reduce(f32[2,2048]{1,0:T(2,128)S(1)} %pad_maximum_fusion.5), channel_id=1, replica_groups=mesh['ids'=8,'mdl'=4] {'ids','mdl'}, use_global_device_ids=true, to_apply=%region_10.11 | all-reduce | flops 4096 | bytes 32768 | tf_op jit(solution)/shard_map/psum | solution.py:198
  315.1 12.7 %multiply_convert_fusion.1 = bf16[1024,2048]{1,0:T(8,128)(2,1)S(1)} fusion(f32[1024,2048]{1,0:T(8,128)} %get-tuple-element.167, f32[1024,2048]{1,0:T(8,128)} %get-tuple-element.165, f32[1024,2048]{1,0:T(8,128)} %get-tuple-element.148, f32[]{:T(128)} %get-tuple-element.125, f32[2048]{0:T(1024)S(1)} %bitcast.120, f32[2048]{0:T(1024)S(1)} %bitcast.119, ...), kind=kLoop, calls=%fused_computation.25 | loop fusion | flops 52428800 | bytes 29405188 | tf_op jit(solution)/shard_map/convert_element_type | solution.py:213
  327.8 18.4 %multiply_reduce_fusion.2 = (f32[2048]{0:T(1024)S(1)}, f32[2048]{0:T(1024)S(1)}, f32[1024,2048]{1,0:T(8,128)}) fusion(f32[2048]{0:T(1024)S(1)} %bitcast.94, f32[2048]{0:T(1024)S(1)} %bitcast.97, f32[1024,2048]{1,0:T(8,128)} %get-tuple-element.164, bf16[1024,2048]{1,0:T(8,128)(2,1)S(1)} %multiply_convert_fusion.1, ...), kind=kOutput, calls=%fused_computation.24 | convolution fusion | flops 8615096320 | bytes 29392896 | tf_op jit(solution)/shard_map/dot_general | solution.py:36
  346.2 40.7 %all-reduce.5 = (f32[2,2048]{1,0:T(2,128)S(1)}, f32[32]{0:T(128)S(1)}) all-reduce(f32[2,2048]{1,0:T(2,128)S(1)} %pad_maximum_fusion.6, f32[32]{0:T(128)S(1)} %get-tuple-element.144), channel_id=1, replica_groups=mesh['ids'=8,'mdl'=4] {'ids','mdl'}, use_global_device_ids=true, to_apply=%region_13.14 | all-reduce | flops 4128 | bytes 33024 | tf_op jit(solution)/shard_map/psum | solution.py:224
  386.9 11.3 %multiply_convert_fusion = bf16[1024,2048]{1,0:T(8,128)(2,1)S(1)} fusion(f32[1024,2048]{1,0:T(8,128)} %get-tuple-element.168, f32[1024,2048]{1,0:T(8,128)} %get-tuple-element.164, f32[2048]{0:T(1024)S(1)} %bitcast.114, f32[2048]{0:T(1024)S(1)} %bitcast.113, f32[]{:T(128)} %get-tuple-element.125, f32[2048]{0:T(1024)S(1)} %bitcast.95, f32[2048]{0:T(1024)S(1)} %bitcast.98, ...), kind=kLoop, calls=%fused_computation.23 | loop fusion | flops 54525952 | bytes 21016580 | tf_op jit(solution)/shard_map/convert_element_type | solution.py:242
  403.2 3.7 pad_maximum_fusion.1
  407.2 5.1 convolution_bitcast_fusion
  412.3 2.4 convolution_bitcast_fusion.1
  414.7 2.4 convolution_bitcast_fusion.2
  417.0 2.4 convolution_bitcast_fusion.3
  419.4 6.5 pad_maximum_fusion
  426.1 5.7 fusion.32
  431.8 47.1 %reduce-scatter.4.cloned.1.call-done = f32[1,1024,512]{2,1,0:T(8,128)} async-done(((f32[4,1024,512]{2,1,0:T(8,128)}), f32[1,1024,512]{2,1,0:T(8,128)}) %reduce-scatter.4.cloned.1.call-update) | async-done | bytes 2097168 | tf_op jit(solution)/shard_map/reduce_scatter | solution.py:249
  479.0 127.4 %reduce-scatter.8.cloned.1.call-done = f32[1,2048,512]{2,1,0:T(8,128)} async-done(((f32[4,2048,512]{2,1,0:T(8,128)}), f32[1,2048,512]{2,1,0:T(8,128)}) %reduce-scatter.8.cloned.1.call-update) | async-done | bytes 4194320 | tf_op jit(solution)/shard_map/reduce_scatter | solution.py:220
  607.7 6.0 all_gather.33
  613.7 6.8 fusion.18
  623.3 5.5 all-to-all-start.3
  630.0 109.6 %all-reduce.12.cloned.1.call-done = f32[2048,32]{0,1:T(8,128)} async-done(((f32[2048,32]{0,1:T(8,128)}), f32[2048,32]{0,1:T(8,128)}) %all-reduce.12.cloned.1.call-update) | async-done | bytes 262160 | tf_op jit(solution)/shard_map/psum | solution.py:224
  742.6 15.7 %all_gather.34 = bf16[8,1024,32]{2,1,0:T(8,128)(2,1)S(1)} all-gather(bf16[8,256,32]{2,1,0:T(8,128)(2,1)S(1)} %reshape.98), channel_id=1, replica_groups=mesh['ids'=8,'mdl'=4] {'mdl'}, dimensions={1}, use_global_device_ids=true | all-gather | bytes 655360 | tf_op jit(solution)/shard_map/all_gather | solution.py:185
  758.3 14.1 %fusion.19 = bf16[2048,32]{0,1:T(8,128)(2,1)S(1)} fusion(bf16[8192,32]{1,0:T(8,128)(2,1)S(1)} %bitcast.83, s32[2048]{0:T(1024)S(1)} %dynamic-slice-done), kind=kOutput, calls=%fused_computation.48 | convolution fusion | flops 1090584576 | bytes 663552 | tf_op jit(solution)/shard_map/dot_general | solution.py:192
  772.4 7.5 all_gather.35
  779.9 30.7 %reduce-scatter.6.cloned.1.call-done = f32[128,512]{1,0:T(8,128)} async-done(((f32[1024,512]{1,0:T(8,128)}), f32[128,512]{1,0:T(8,128)}) %reduce-scatter.6.cloned.1.call-update) | async-done | bytes 262160 | tf_op jit(solution)/shard_map/reduce_scatter | solution.py:250
  815.0 154.8 %all-reduce.10.cloned.1.call-done = f32[4,512,512]{2,1,0:T(8,128)} async-done(((f32[4,512,512]{2,1,0:T(8,128)}), f32[4,512,512]{2,1,0:T(8,128)}) %all-reduce.10.cloned.1.call-update) | async-done | bytes 4194320 | tf_op jit(solution)/shard_map/psum | solution.py:221
  969.8 4.3 slice.126
  974.1 4.3 reshape.103
  978.3 5.2 copy.103
  983.5 9.0 fusion.48
  (132 shorter events, 33.7 us)
Async XLA Ops:
  7.2 2.6 copy-start
  7.2 46.1 %all-gather.5.cloned.1.call-start = ((), (), s32[]{:S(2)}) async-start(), calls=%async_computation.7 | async-start | bytes 1179648 | tf_op jit(solution)/shard_map/all_gather | solution.py:109
  9.0 129.6 %all-gather.9.cloned.1.call-start = ((), (), s32[]{:S(2)}) async-start(), calls=%async_computation.9 | async-start | bytes 1310720 | tf_op jit(solution)/shard_map/all_gather | solution.py:142
  48.2 98.8 %all-gather.7.cloned.1.call-start = ((), (), s32[]{:S(2)}) async-start(), calls=%async_computation.8 | async-start | bytes 5242880 | tf_op jit(solution)/shard_map/all_gather | solution.py:110
  53.3 12.3 %copy-start.17 = (s32[8,1024]{1,0:T(8,128)S(1)}, s32[8,1024]{1,0:T(8,128)}, u32[]{:S(2)}) copy-start(s32[8,1024]{1,0:T(8,128)} %param.21) | copy-start | bytes 98308
  53.3 12.3 %copy-start.20 = (s32[8]{0:T(128)S(1)}, s32[8]{0:T(128)}, u32[]{:S(2)}) copy-start(s32[8]{0:T(128)} %param.22) | copy-start | bytes 100
  53.3 152.9 %all-gather.11.cloned.1.call-start = ((), (), s32[]{:S(2)}) async-start(), calls=%async_computation.10 | async-start | bytes 10485760 | tf_op jit(solution)/shard_map/all_gather | solution.py:115
  63.5 18.1 %copy-start.8 = (f32[450,32]{0,1:T(8,128)S(1)}, f32[450,32]{0,1:T(8,128)}, u32[]{:S(2)}) copy-start(f32[450,32]{0,1:T(8,128)} %param.27) | copy-start | bytes 172804
  63.5 18.2 %copy-start.15 = (f32[4,450]{1,0:T(4,128)S(1)}, f32[4,450]{1,0:T(4,128)}, u32[]{:S(2)}) copy-start(f32[4,450]{1,0:T(4,128)} %param.28) | copy-start | bytes 21604
  66.3 11.7 %all-to-all-start = ((s32[8,1,1024]{2,1,0:T(1,128)}), s32[8,1,1024]{2,1,0:T(1,128)S(1)}, u32[]{:S(2)}, u32[]{:S(2)}) async-start(s32[8,1,1024]{2,1,0:T(1,128)} %all_to_all.32), calls=%async_computation | async-start | bytes 65536 | tf_op jit(solution)/shard_map/all_to_all | solution.py:127
  78.0 68.4 %copy-start.12 = (s32[8,1,1024]{2,1,0:T(1,128)}, s32[8,1,1024]{2,1,0:T(1,128)S(1)}, u32[]{:S(2)}) copy-start(s32[8,1,1024]{2,1,0:T(1,128)S(1)} %all-to-all-done) | copy-start | bytes 98308
  78.0 58.2 %all-to-all-start.1 = ((bf16[4,1024,256]{2,1,0:T(8,128)(2,1)}), bf16[4,1024,256]{2,1,0:T(8,128)(2,1)S(1)}, u32[]{:S(2)}, u32[]{:S(2)}) async-start(bf16[4,1024,256]{2,1,0:T(8,128)(2,1)} %bitcast.3), calls=%async_computation.1 | async-start | bytes 4194304 | tf_op jit(solution)/shard_map/all_to_all | solution.py:120
  81.6 397.3 %reduce-scatter.4.cloned.1.call-start = ((), (), s32[]{:S(2)}) async-start(), calls=%async_computation.11 | async-start | bytes 10485760 | tf_op jit(solution)/shard_map/reduce_scatter | solution.py:249
  140.1 6.9 copy-start.6
  206.2 59.3 %copy-start.21 = (f32[32]{0:T(128)S(1)}, f32[32]{0:T(128)}, u32[]{:S(2)}) copy-start(f32[32]{0:T(128)} %param.29) | copy-start | bytes 388
  264.7 6.0 copy-start.2
  327.8 18.4 %copy-start.4 = (bf16[1024,2048]{1,0:T(8,128)(2,1)}, bf16[1024,2048]{1,0:T(8,128)(2,1)S(1)}, u32[]{:S(2)}) copy-start(bf16[1024,2048]{1,0:T(8,128)(2,1)S(1)} %multiply_convert_fusion.1) | copy-start | bytes 12582916
  406.9 199.5 %reduce-scatter.8.cloned.1.call-start = ((), (), s32[]{:S(2)}) async-start(), calls=%async_computation.13 | async-start | bytes 20971520 | tf_op jit(solution)/shard_map/reduce_scatter | solution.py:220
  407.1 5.1 copy-start.3
  407.1 5.1 copy-start.5
  426.0 180.5 %copy-start.7 = (f32[128,450]{0,1:T(8,128)S(1)}, f32[128,450]{0,1:T(8,128)}, u32[]{:S(2)}) copy-start(f32[128,450]{0,1:T(8,128)} %param.25) | copy-start | bytes 691204
  426.0 180.7 %copy-start.10 = (f32[128,450]{0,1:T(8,128)S(1)}, f32[128,450]{0,1:T(8,128)}, u32[]{:S(2)}) copy-start(f32[128,450]{0,1:T(8,128)} %param.31) | copy-start | bytes 691204
  426.0 180.8 %copy-start.11 = (f32[128,450]{0,1:T(8,128)S(1)}, f32[128,450]{0,1:T(8,128)}, u32[]{:S(2)}) copy-start(f32[128,450]{0,1:T(8,128)} %param.30) | copy-start | bytes 691204
  426.0 313.6 %all-reduce.12.cloned.1.call-start = ((), (), s32[]{:S(2)}) async-start(), calls=%async_computation.15 | async-start | bytes 524288 | tf_op jit(solution)/shard_map/psum | solution.py:224
  431.8 378.8 %reduce-scatter.6.cloned.1.call-start = ((), (), s32[]{:S(2)}) async-start(), calls=%async_computation.12 | async-start | bytes 2359296 | tf_op jit(solution)/shard_map/reduce_scatter | solution.py:250
  478.9 490.8 %all-reduce.10.cloned.1.call-start = ((), (), s32[]{:S(2)}) async-start(), calls=%async_computation.14 | async-start | bytes 8388608 | tf_op jit(solution)/shard_map/psum | solution.py:221
  606.6 22.2 %copy-start.22 = (f32[32]{0:T(128)S(1)}, f32[32]{0:T(128)}, u32[]{:S(2)}) copy-start(f32[32]{0:T(128)} %param.39) | copy-start | bytes 388
  606.6 22.2 %copy-start.23 = (f32[32]{0:T(128)S(1)}, f32[32]{0:T(128)}, u32[]{:S(2)}) copy-start(f32[32]{0:T(128)} %param.38) | copy-start | bytes 388
  606.6 22.7 %copy-start.16 = (f32[4,450]{1,0:T(4,128)S(1)}, f32[4,450]{1,0:T(4,128)}, u32[]{:S(2)}) copy-start(f32[4,450]{1,0:T(4,128)} %param.28) | copy-start | bytes 21604
  606.6 22.7 %copy-start.18 = (f32[4,450]{1,0:T(4,128)S(1)}, f32[4,450]{1,0:T(4,128)}, u32[]{:S(2)}) copy-start(f32[4,450]{1,0:T(4,128)} %param.37) | copy-start | bytes 21604
  606.6 22.7 %copy-start.19 = (f32[4,450]{1,0:T(4,128)S(1)}, f32[4,450]{1,0:T(4,128)}, u32[]{:S(2)}) copy-start(f32[4,450]{1,0:T(4,128)} %param.36) | copy-start | bytes 21604
  606.7 133.0 %copy-start.9 = (f32[450,32]{0,1:T(8,128)S(1)}, f32[450,32]{0,1:T(8,128)}, u32[]{:S(2)}) copy-start(f32[450,32]{0,1:T(8,128)} %param.27) | copy-start | bytes 172804
  606.7 133.0 %copy-start.13 = (f32[450,32]{0,1:T(8,128)S(1)}, f32[450,32]{0,1:T(8,128)}, u32[]{:S(2)}) copy-start(f32[450,32]{0,1:T(8,128)} %param.35) | copy-start | bytes 172804
  606.7 133.0 %copy-start.14 = (f32[450,32]{0,1:T(8,128)S(1)}, f32[450,32]{0,1:T(8,128)}, u32[]{:S(2)}) copy-start(f32[450,32]{0,1:T(8,128)} %param.34) | copy-start | bytes 172804
  613.7 144.6 %dynamic-slice-start = ((s32[8192]{0:T(1024)}, s32[]{:T(128)}), s32[2048]{0:T(1024)S(1)}, s32[]{:S(2)}) async-start(s32[8192]{0:T(1024)} %param.23, s32[]{:T(128)} %select_n.30), calls=%async_computation.16 | async-start | bytes 16896 | tf_op jit(solution)/shard_map/dynamic_slice | solution.py:187
  623.3 118.1 %all-to-all-start.3 = ((bf16[8,2,4096]{2,1,0:T(2,128)(2,1)}), bf16[8,2,4096]{2,1,0:T(2,128)(2,1)S(1)}, u32[]{:S(2)}, u32[]{:S(2)}) async-start(bf16[8,2,4096]{2,1,0:T(2,128)(2,1)} %reshape.109), calls=%async_computation.3 | async-start | bytes 262144 | tf_op jit(solution)/shard_map/all_to_all | solution.py:184
  978.3 14.9 %copy-start.1 = (bf16[8192,32]{0,1:T(8,128)(2,1)S(1)}, bf16[8192,32]{0,1:T(8,128)(2,1)}, u32[]{:S(2)}) copy-start(bf16[8192,32]{0,1:T(8,128)(2,1)} %param.24) | copy-start | bytes 1572868
Sparse Core Ops, SparseCore 0:
  10.6 42.5 all-gather.4
  55.4 17.2 all-gather.8
  74.3 56.9 all-gather.6
  133.3 57.1 all-gather.10
  407.0 71.8 reduce-scatter.3
  481.3 125.0 reduce-scatter.7
  612.5 127.0 all-reduce.11
  743.2 67.4 reduce-scatter.5
  814.3 155.4 all-reduce.9
where the time goes:
time: 1010 us; the launch traced here: 1000 us
  waiting for transfers between devices  477 us (47%)
  blocking collectives  262 us (26%)
  matrix products  121 us (12%)
  other arithmetic  72.2 us (7%)
  local copies, waits for them, and re-layouts  37.4 us (4%)
  between operations  15.7 us (2%)
  starting transfers between devices  15 us (1%)
    psum x1, waiting for transfers between devices, body(): grad_second = lax.psum(grad_second, 'ids')  155 us
    reduce_scatter x1, waiting for transfers between devices, body(): lax.psum_scatter(local_second, 'mdl', scatter_dimension=0, tiled=False)  127 us
    psum x1, waiting for transfers between devices, body(): lax.psum((jnp.stack([jnp.sum(incoming_one * unit_one, 0), jnp.sum(incomin...  110 us
    all_gather x1, blocking collectives, body(): lax.all_gather(jnp.pad(norm_params, ((0, 0), (0, more))), 'mdl', axis=1,...  48.9 us
    reduce_scatter x1, waiting for transfers between devices, body(): lax.psum_scatter(local_first, 'mdl', scatter_dimension=0, tiled=False)  47.1 us
    dot_general x11, matrix products, contract(): lax.dot_general(left, right, (((left_dim,), (right_dim,)), ((), ())), pre...  45.5 us
    psum x1, blocking collectives, body(): lax.psum((jnp.stack([jnp.sum(incoming_one * unit_one, 0), jnp.sum(incomin...  40.7 us
    psum x1, blocking collectives, body(): lax.psum(jnp.stack([jnp.sum(incoming_two * unit_two, 0), jnp.sum(incoming...  40.2 us
  transfers between devices with their start and end apart: 12, of which 7 were waited for; matrix products, arithmetic and copies ran while one was open for 12% of the time, Pallas kernels for 0%

commit v1 on v0

--- a/solution.py
+++ b/solution.py
@@ -218,7 +218,11 @@
         ]
     )
     grad_second = lax.psum_scatter(local_second, "mdl", scatter_dimension=0, tiled=False)
-    grad_second = lax.psum(grad_second, "ids")
+    grad_second = grad_second
+    for hop in (1, 2, 4):
+        grad_second = grad_second + lax.ppermute(
+            grad_second, "ids", [(dev, dev ^ hop) for dev in range(8)]
+        )
     grad_second = grad_second.reshape(parts, wide, wide)[:, :width, :width].reshape(-1, width)
     incoming_one = contract(grad_linear_two, second_low, 1, 1)
     sums_one, final_sum, grad_bias = lax.psum(

time: 1010 us -> 972 us (0.962)
  waiting for transfers between devices: 477 us -> 423 us
  other arithmetic: 72.2 us -> 88.1 us
    ppermute x0 -> x3, waiting for transfers between devices: none -> 177 us  [body(): lax.ppermute(grad_second, 'ids', [(dev, dev ^ hop) for dev in range(8)])]
    psum x1 -> x0, waiting for transfers between devices: 155 us -> none  [body(): grad_second = lax.psum(grad_second, 'ids')]
    reduce_scatter x1, waiting for transfers between devices: 127 us -> 45.1 us  [body(): lax.psum_scatter(local_second, 'mdl', scatter_dimension=0, tiled=False)]
    psum x1, waiting for transfers between devices: 110 us -> 160 us  [body(): lax.psum((jnp.stack([jnp.sum(incoming_one * unit_one, 0), jnp.sum(incomin...]
    reduce_scatter x1, waiting for transfers between devices: 47.1 us -> 0.02 us  [body(): lax.psum_scatter(local_first, 'mdl', scatter_dimension=0, tiled=False)]
    add x0 -> x3, other arithmetic: none -> 16 us  [body(): grad_second + lax.ppermute(grad_second, 'ids', [(dev, dev ^ hop) for dev...]
  transfers between devices with their start and end apart: 12 -> 14, of which waited for: 7 -> 7; matrix products, arithmetic and copies ran while one was open for 12% -> 16% of each run, Pallas kernels for 0% -> 0%
where the time goes in v1:
time: 972 us; the launch traced here: 963 us
  waiting for transfers between devices  423 us (44%)
  blocking collectives  263 us (27%)
  matrix products  118 us (12%)
  other arithmetic  88.1 us (9%)
  local copies, waits for them, and re-layouts  35.4 us (4%)
  starting transfers between devices  18.8 us (2%)
  between operations  15.9 us (2%)
    ppermute x3, waiting for transfers between devices, body(): lax.ppermute(grad_second, 'ids', [(dev, dev ^ hop) for dev in range(8)])  177 us
    psum x1, waiting for transfers between devices, body(): lax.psum((jnp.stack([jnp.sum(incoming_one * unit_one, 0), jnp.sum(incomin...  160 us
    all_gather x1, blocking collectives, body(): lax.all_gather(jnp.pad(norm_params, ((0, 0), (0, more))), 'mdl', axis=1,...  48.9 us
    reduce_scatter x1, waiting for transfers between devices, body(): lax.psum_scatter(local_second, 'mdl', scatter_dimension=0, tiled=False)  45.1 us
    dot_general x11, matrix products, contract(): lax.dot_general(left, right, (((left_dim,), (right_dim,)), ((), ())), pre...  43.2 us
    psum x1, blocking collectives, body(): lax.psum((jnp.stack([jnp.sum(incoming_one * unit_one, 0), jnp.sum(incomin...  41.6 us
    psum x1, blocking collectives, body(): lax.psum(jnp.stack([jnp.sum(incoming_two * unit_two, 0), jnp.sum(incoming...  40.4 us
    psum x1, blocking collectives, body(): lax.psum(jnp.stack([jnp.sum(weighted_two, 0), jnp.sum(weighted_two * acti...  40.1 us
  transfers between devices with their start and end apart: 14, of which 7 were waited for; matrix products, arithmetic and copies ran while one was open for 16% of the time, Pallas kernels for 0%

profile of v1, /device:TPU:0, one launch (start us, length us, event | category | flops | bytes accessed | tf_op | source)
XLA Modules:
  0.0 963.1 jit_solution(8352940345309662464)
XLA Ops:
  9.8 13.0 %subtract_convert_fusion = (bf16[2048,32]{0,1:T(8,128)(2,1)S(1)}, bf16[2048,32]{0,1:T(8,128)(2,1)S(1)}) fusion(bf16[8192,32]{0,1:T(8,128)(2,1)S(1)} %copy-done, s32[8192]{0:T(1024)S(1)} %fusion.37), kind=kOutput, calls=%fused_computation.68 | convolution fusion | flops 1090846720 | bytes 819200 | tf_op jit(solution)/shard_map/dot_general | solution.py:134
  26.4 18.5 %all_to_all.48 = bf16[8,2,8192]{2,1,0:T(2,128)(2,1)S(1)} all-to-all(bf16[8,2,8192]{2,1,0:T(2,128)(2,1)S(1)} %reshape.106), channel_id=1, replica_groups=mesh['ids'=8,'mdl'=4] {'ids'}, dimensions={0} | all-to-all | bytes 524288 | tf_op jit(solution)/shard_map/all_to_all | solution.py:141
  48.2 5.1 all-gather.5.cloned.1.call-done
  53.7 3.4 convert_element_type.79
  57.1 5.6 reshape.96
  66.3 5.0 all-to-all-start
  71.3 4.1 add_convert_fusion.2
  75.4 2.6 all-to-all-done
  78.0 3.7 all-to-all-start.1
  81.7 48.9 %all_gather.27 = f32[4,2048]{1,0:T(4,128)S(1)} all-gather(f32[4,512]{1,0:T(4,128)S(1)} %pad.17), channel_id=1, replica_groups=mesh['ids'=8,'mdl'=4] {'mdl'}, dimensions={1}, use_global_device_ids=true | all-gather | bytes 40960 | tf_op jit(solution)/shard_map/all_gather | solution.py:118
  130.7 5.4 all_gather.32
  140.1 6.3 fusion.4
  147.0 11.5 %multiply_reduce_fusion.1 = (f32[2048]{0:T(1024)S(1)}, f32[2048]{0:T(1024)S(1)}, f32[1024,2048]{1,0:T(8,128)}) fusion(f32[1024]{0:T(1024)S(1)} %bitcast.112, bf16[1024,1024]{0,1:T(8,128)(2,1)S(1)} %bitcast.88, bf16[1024,2048]{0,1:T(8,128)(2,1)} %all-gather.7.cloned.1.call-done), kind=kOutput, calls=%fused_computation.19 | convolution fusion | flops 4318031872 | bytes 14700544 | tf_op jit(solution)/shard_map/dot_general | solution.py:156
  158.5 39.1 %all-reduce.6 = (f32[2,2048]{1,0:T(2,128)S(1)}, f32[]{:T(128)}) all-reduce(f32[2,2048]{1,0:T(2,128)S(1)} %pad_maximum_fusion.3, f32[]{:T(128)} %get-tuple-element.151), channel_id=1, replica_groups=mesh['ids'=8,'mdl'=4] {'ids','mdl'}, use_global_device_ids=true, to_apply=%region_2.3 | all-reduce | flops 4097 | bytes 32776 | tf_op jit(solution)/shard_map/psum | solution.py:160
  198.9 7.3 add_convert_fusion.1
  206.2 18.4 %multiply_reduce_fusion = (f32[2048]{0:T(1024)S(1)}, f32[2048]{0:T(1024)S(1)}, f32[1024,2048]{1,0:T(8,128)}, f32[1024,2048]{1,0:T(8,128)}) fusion(f32[1024]{0:T(1024)S(1)} %bitcast.113, bf16[1024,2048]{1,0:T(8,128)(2,1)} %add_convert_fusion.1, bf16[2048,2048]{0,1:T(8,128)(2,1)} %all-gather.11.cloned.1.call-done), kind=kOutput, calls=%fused_computation.17 | convolution fusion | flops 8612999168 | bytes 29380608 | tf_op jit(solution)/shard_map/dot_general | solution.py:165
  224.6 40.1 %psum.51 = f32[2,2048]{1,0:T(2,128)S(1)} all-reduce(f32[2,2048]{1,0:T(2,128)S(1)} %pad_maximum_fusion.4), channel_id=1, replica_groups=mesh['ids'=8,'mdl'=4] {'ids','mdl'}, use_global_device_ids=true, to_apply=%region_7.8 | all-reduce | flops 4096 | bytes 32768 | tf_op jit(solution)/shard_map/psum | solution.py:168
  265.6 5.1 convert_reduce_fusion
  270.8 4.2 multiply_reduce_fusion.3
  275.0 40.4 %psum.52 = f32[2,2048]{1,0:T(2,128)S(1)} all-reduce(f32[2,2048]{1,0:T(2,128)S(1)} %pad_maximum_fusion.5), channel_id=1, replica_groups=mesh['ids'=8,'mdl'=4] {'ids','mdl'}, use_global_device_ids=true, to_apply=%region_10.11 | all-reduce | flops 4096 | bytes 32768 | tf_op jit(solution)/shard_map/psum | solution.py:198
  315.4 13.0 %multiply_convert_fusion.1 = bf16[1024,2048]{1,0:T(8,128)(2,1)S(1)} fusion(f32[1024,2048]{1,0:T(8,128)} %get-tuple-element.167, f32[1024,2048]{1,0:T(8,128)} %get-tuple-element.165, f32[1024,2048]{1,0:T(8,128)} %get-tuple-element.148, f32[]{:T(128)} %get-tuple-element.125, f32[2048]{0:T(1024)S(1)} %bitcast.123, f32[2048]{0:T(1024)S(1)} %bitcast.122, ...), kind=kLoop, calls=%fused_computation.25 | loop fusion | flops 52428800 | bytes 29405188 | tf_op jit(solution)/shard_map/convert_element_type | solution.py:213
  328.5 2.5 convolution_bitcast_fusion
  330.9 2.4 convolution_bitcast_fusion.1
  333.3 2.4 convolution_bitcast_fusion.2
  338.1 6.1 pad_maximum_fusion
  344.3 18.9 %multiply_reduce_fusion.2 = (f32[2048]{0:T(1024)S(1)}, f32[2048]{0:T(1024)S(1)}, f32[1024,2048]{1,0:T(8,128)}) fusion(f32[2048]{0:T(1024)S(1)} %bitcast.97, f32[2048]{0:T(1024)S(1)} %bitcast.100, f32[1024,2048]{1,0:T(8,128)} %get-tuple-element.164, bf16[1024,2048]{1,0:T(8,128)(2,1)} %copy-done.4, bf16[2048,2048]{0,1:T(8,128)(2,1)} %all-gather.11.cloned.1.call-done), kind=kOutput, calls=%fused_computation.24 | convolution fusion | flops 8615096320 | bytes 29392896 | tf_op jit(solution)/shard_map/dot_general | solution.py:36
  363.2 41.6 %all-reduce.5 = (f32[2,2048]{1,0:T(2,128)S(1)}, f32[32]{0:T(128)S(1)}) all-reduce(f32[2,2048]{1,0:T(2,128)S(1)} %pad_maximum_fusion.6, f32[32]{0:T(128)S(1)} %get-tuple-element.144), channel_id=1, replica_groups=mesh['ids'=8,'mdl'=4] {'ids','mdl'}, use_global_device_ids=true, to_apply=%region_13.14 | all-reduce | flops 4128 | bytes 33024 | tf_op jit(solution)/shard_map/psum | solution.py:228
  404.9 11.2 %multiply_convert_fusion = bf16[1024,2048]{1,0:T(8,128)(2,1)S(1)} fusion(f32[1024,2048]{1,0:T(8,128)} %get-tuple-element.168, f32[1024,2048]{1,0:T(8,128)} %get-tuple-element.164, f32[2048]{0:T(1024)S(1)} %bitcast.117, f32[2048]{0:T(1024)S(1)} %bitcast.116, f32[]{:T(128)} %get-tuple-element.125, f32[2048]{0:T(1024)S(1)} %bitcast.98, f32[2048]{0:T(1024)S(1)} %bitcast.101, ...), kind=kLoop, calls=%fused_computation.23 | loop fusion | flops 54525952 | bytes 21016580 | tf_op jit(solution)/shard_map/convert_element_type | solution.py:246
  421.1 3.7 pad_maximum_fusion.1
  424.8 45.1 %reduce-scatter.8.cloned.1.call-done = f32[1,2048,512]{2,1,0:T(8,128)} async-done(((f32[4,2048,512]{2,1,0:T(8,128)}), f32[1,2048,512]{2,1,0:T(8,128)}) %reduce-scatter.8.cloned.1.call-update) | async-done | bytes 4194320 | tf_op jit(solution)/shard_map/reduce_scatter | solution.py:220
  471.3 91.0 %collective-permute-done = f32[2048,512]{1,0:T(8,128)S(1)} collective-permute-done((f32[2048,512]{1,0:T(8,128)}, f32[2048,512]{1,0:T(8,128)S(1)}, u32[]{:S(2)}, u32[]{:S(2)}) %collective-permute-start) | collective-permute-done | bytes 4194336 | tf_op jit(solution)/shard_map/ppermute | solution.py:223
  562.3 5.1 bitcast_add_fusion
  568.9 5.6 fusion.32
  575.3 85.8 %collective-permute-done.1 = f32[2048,512]{1,0:T(8,128)} collective-permute-done((f32[2048,512]{1,0:T(8,128)}, f32[2048,512]{1,0:T(8,128)}, u32[]{:S(2)}, u32[]{:S(2)}) %collective-permute-start.1) | collective-permute-done | bytes 4194336 | tf_op jit(solution)/shard_map/ppermute | solution.py:223
  661.1 6.4 add.278
  667.5 2.6 collective-permute-start.2
  671.4 5.8 all_gather.33
  677.1 6.8 fusion.18
  686.7 3.8 all-to-all-start.3
  691.8 159.9 %all-reduce.9.cloned.1.call-done = f32[2048,32]{0,1:T(8,128)} async-done(((f32[2048,32]{0,1:T(8,128)}), f32[2048,32]{0,1:T(8,128)}) %all-reduce.9.cloned.1.call-update) | async-done | bytes 262160 | tf_op jit(solution)/shard_map/psum | solution.py:228
  854.7 16.1 %all_gather.34 = bf16[8,1024,32]{2,1,0:T(8,128)(2,1)S(1)} all-gather(bf16[8,256,32]{2,1,0:T(8,128)(2,1)S(1)} %reshape.98), channel_id=1, replica_groups=mesh['ids'=8,'mdl'=4] {'mdl'}, dimensions={1}, use_global_device_ids=true | all-gather | bytes 655360 | tf_op jit(solution)/shard_map/all_gather | solution.py:185
  870.8 14.1 %fusion.19 = bf16[2048,32]{0,1:T(8,128)(2,1)S(1)} fusion(bf16[8192,32]{1,0:T(8,128)(2,1)S(1)} %bitcast.86, s32[2048]{0:T(1024)S(1)} %dynamic-slice-done), kind=kOutput, calls=%fused_computation.48 | convolution fusion | flops 1090584576 | bytes 663552 | tf_op jit(solution)/shard_map/dot_general | solution.py:192
  884.9 7.5 all_gather.35
  892.4 33.0 %reduce-scatter.6.cloned.1.call-done = f32[128,512]{1,0:T(8,128)} async-done(((f32[1024,512]{1,0:T(8,128)}), f32[128,512]{1,0:T(8,128)}) %reduce-scatter.6.cloned.1.call-update) | async-done | bytes 262160 | tf_op jit(solution)/shard_map/reduce_scatter | solution.py:254
  929.8 4.5 add.279
  936.5 4.3 reshape.102
  940.9 5.2 copy.103
  946.0 9.0 fusion.48
  (136 shorter events, 46.1 us)
Async XLA Ops:
  7.2 2.6 copy-start
  7.2 46.1 %all-gather.5.cloned.1.call-start = ((), (), s32[]{:S(2)}) async-start(), calls=%async_computation.7 | async-start | bytes 1179648 | tf_op jit(solution)/shard_map/all_gather | solution.py:109
  9.0 129.6 %all-gather.9.cloned.1.call-start = ((), (), s32[]{:S(2)}) async-start(), calls=%async_computation.9 | async-start | bytes 1310720 | tf_op jit(solution)/shard_map/all_gather | solution.py:142
  48.2 98.8 %all-gather.7.cloned.1.call-start = ((), (), s32[]{:S(2)}) async-start(), calls=%async_computation.8 | async-start | bytes 5242880 | tf_op jit(solution)/shard_map/all_gather | solution.py:110
  53.3 12.3 %copy-start.16 = (s32[8,1024]{1,0:T(8,128)S(1)}, s32[8,1024]{1,0:T(8,128)}, u32[]{:S(2)}) copy-start(s32[8,1024]{1,0:T(8,128)} %param.21) | copy-start | bytes 98308
  53.3 12.3 %copy-start.19 = (s32[8]{0:T(128)S(1)}, s32[8]{0:T(128)}, u32[]{:S(2)}) copy-start(s32[8]{0:T(128)} %param.22) | copy-start | bytes 100
  53.3 152.9 %all-gather.11.cloned.1.call-start = ((), (), s32[]{:S(2)}) async-start(), calls=%async_computation.10 | async-start | bytes 10485760 | tf_op jit(solution)/shard_map/all_gather | solution.py:115
  63.5 18.1 %copy-start.7 = (f32[450,32]{0,1:T(8,128)S(1)}, f32[450,32]{0,1:T(8,128)}, u32[]{:S(2)}) copy-start(f32[450,32]{0,1:T(8,128)} %param.27) | copy-start | bytes 172804
  63.5 18.2 %copy-start.14 = (f32[4,450]{1,0:T(4,128)S(1)}, f32[4,450]{1,0:T(4,128)}, u32[]{:S(2)}) copy-start(f32[4,450]{1,0:T(4,128)} %param.28) | copy-start | bytes 21604
  66.3 11.7 %all-to-all-start = ((s32[8,1,1024]{2,1,0:T(1,128)}), s32[8,1,1024]{2,1,0:T(1,128)S(1)}, u32[]{:S(2)}, u32[]{:S(2)}) async-start(s32[8,1,1024]{2,1,0:T(1,128)} %all_to_all.32), calls=%async_computation | async-start | bytes 65536 | tf_op jit(solution)/shard_map/all_to_all | solution.py:127
  78.0 68.4 %copy-start.11 = (s32[8,1,1024]{2,1,0:T(1,128)}, s32[8,1,1024]{2,1,0:T(1,128)S(1)}, u32[]{:S(2)}) copy-start(s32[8,1,1024]{2,1,0:T(1,128)S(1)} %all-to-all-done) | copy-start | bytes 98308
  78.0 58.2 %all-to-all-start.1 = ((bf16[4,1024,256]{2,1,0:T(8,128)(2,1)}), bf16[4,1024,256]{2,1,0:T(8,128)(2,1)S(1)}, u32[]{:S(2)}, u32[]{:S(2)}) async-start(bf16[4,1024,256]{2,1,0:T(8,128)(2,1)} %bitcast.3), calls=%async_computation.1 | async-start | bytes 4194304 | tf_op jit(solution)/shard_map/all_to_all | solution.py:120
  81.6 388.3 %reduce-scatter.8.cloned.1.call-start = ((), (), s32[]{:S(2)}) async-start(), calls=%async_computation.13 | async-start | bytes 20971520 | tf_op jit(solution)/shard_map/reduce_scatter | solution.py:220
  140.1 6.9 copy-start.5
  206.2 59.4 %copy-start.20 = (f32[32]{0:T(128)S(1)}, f32[32]{0:T(128)}, u32[]{:S(2)}) copy-start(f32[32]{0:T(128)} %param.29) | copy-start | bytes 388
  264.8 6.0 copy-start.2
  315.4 13.1 %copy-start.3 = (bf16[1024,2048]{1,0:T(8,128)(2,1)S(1)}, bf16[1024,2048]{1,0:T(8,128)(2,1)}, u32[]{:S(2)}) copy-start(bf16[1024,2048]{1,0:T(8,128)(2,1)} %add_convert_fusion.1) | copy-start | bytes 12582916
  328.5 7.3 copy-start.4
  344.3 230.5 %reduce-scatter.4.cloned.1.call-start = ((), (), s32[]{:S(2)}) async-start(), calls=%async_computation.11 | async-start | bytes 10485760 | tf_op jit(solution)/shard_map/reduce_scatter | solution.py:253
  424.8 426.9 %all-reduce.9.cloned.1.call-start = ((), (), s32[]{:S(2)}) async-start(), calls=%async_computation.14 | async-start | bytes 524288 | tf_op jit(solution)/shard_map/psum | solution.py:228
  469.9 92.4 %collective-permute-start = (f32[2048,512]{1,0:T(8,128)}, f32[2048,512]{1,0:T(8,128)S(1)}, u32[]{:S(2)}, u32[]{:S(2)}) collective-permute-start(f32[2048,512]{1,0:T(8,128)} %bitcast.85), channel_id=1, source_target_pairs={{0,4},{4,0},{8,12},{12,8},{16,20},{20,16},{24,28},{28,24},{1,5},{5... | collective-permute-start | bytes 12582920 | tf_op jit(solution)/shard_map/ppermute | solution.py:223
  567.5 93.6 %collective-permute-start.1 = (f32[2048,512]{1,0:T(8,128)}, f32[2048,512]{1,0:T(8,128)}, u32[]{:S(2)}, u32[]{:S(2)}) collective-permute-start(f32[2048,512]{1,0:T(8,128)} %bitcast_add_fusion), channel_id=1, source_target_pairs={{0,8},{4,12},{8,0},{12,4},{16,24},{20,28},{24,16},{28,20},{1,9},{5... | collective-permute-start | bytes 12582920 | tf_op jit(solution)/shard_map/ppermute | solution.py:223
  574.5 95.6 %copy-start.6 = (f32[128,450]{0,1:T(8,128)S(1)}, f32[128,450]{0,1:T(8,128)}, u32[]{:S(2)}) copy-start(f32[128,450]{0,1:T(8,128)} %param.25) | copy-start | bytes 691204
  574.5 95.9 %copy-start.9 = (f32[128,450]{0,1:T(8,128)S(1)}, f32[128,450]{0,1:T(8,128)}, u32[]{:S(2)}) copy-start(f32[128,450]{0,1:T(8,128)} %param.31) | copy-start | bytes 691204
  574.5 96.0 %copy-start.10 = (f32[128,450]{0,1:T(8,128)S(1)}, f32[128,450]{0,1:T(8,128)}, u32[]{:S(2)}) copy-start(f32[128,450]{0,1:T(8,128)} %param.30) | copy-start | bytes 691204
  574.5 350.9 %reduce-scatter.6.cloned.1.call-start = ((), (), s32[]{:S(2)}) async-start(), calls=%async_computation.12 | async-start | bytes 2359296 | tf_op jit(solution)/shard_map/reduce_scatter | solution.py:254
  667.5 262.3 %collective-permute-start.2 = (f32[2048,512]{1,0:T(8,128)}, f32[2048,512]{1,0:T(8,128)}, u32[]{:S(2)}, u32[]{:S(2)}) collective-permute-start(f32[2048,512]{1,0:T(8,128)} %add.278), channel_id=1, source_target_pairs={{0,16},{4,20},{8,24},{12,28},{16,0},{20,4},{24,8},{28,12},{1,17},{... | collective-permute-start | bytes 12582920 | tf_op jit(solution)/shard_map/ppermute | solution.py:223
  670.3 20.3 %copy-start.21 = (f32[32]{0:T(128)S(1)}, f32[32]{0:T(128)}, u32[]{:S(2)}) copy-start(f32[32]{0:T(128)} %param.39) | copy-start | bytes 388
  670.3 20.3 %copy-start.22 = (f32[32]{0:T(128)S(1)}, f32[32]{0:T(128)}, u32[]{:S(2)}) copy-start(f32[32]{0:T(128)} %param.38) | copy-start | bytes 388
  670.3 20.8 %copy-start.15 = (f32[4,450]{1,0:T(4,128)S(1)}, f32[4,450]{1,0:T(4,128)}, u32[]{:S(2)}) copy-start(f32[4,450]{1,0:T(4,128)} %param.28) | copy-start | bytes 21604
  670.3 20.8 %copy-start.17 = (f32[4,450]{1,0:T(4,128)S(1)}, f32[4,450]{1,0:T(4,128)}, u32[]{:S(2)}) copy-start(f32[4,450]{1,0:T(4,128)} %param.37) | copy-start | bytes 21604
  670.3 20.8 %copy-start.18 = (f32[4,450]{1,0:T(4,128)S(1)}, f32[4,450]{1,0:T(4,128)}, u32[]{:S(2)}) copy-start(f32[4,450]{1,0:T(4,128)} %param.36) | copy-start | bytes 21604
  670.3 181.4 %copy-start.8 = (f32[450,32]{0,1:T(8,128)S(1)}, f32[450,32]{0,1:T(8,128)}, u32[]{:S(2)}) copy-start(f32[450,32]{0,1:T(8,128)} %param.27) | copy-start | bytes 172804
  670.3 181.4 %copy-start.12 = (f32[450,32]{0,1:T(8,128)S(1)}, f32[450,32]{0,1:T(8,128)}, u32[]{:S(2)}) copy-start(f32[450,32]{0,1:T(8,128)} %param.35) | copy-start | bytes 172804
  670.3 181.4 %copy-start.13 = (f32[450,32]{0,1:T(8,128)S(1)}, f32[450,32]{0,1:T(8,128)}, u32[]{:S(2)}) copy-start(f32[450,32]{0,1:T(8,128)} %param.34) | copy-start | bytes 172804
  677.1 193.6 %dynamic-slice-start = ((s32[8192]{0:T(1024)}, s32[]{:T(128)}), s32[2048]{0:T(1024)S(1)}, s32[]{:S(2)}) async-start(s32[8192]{0:T(1024)} %param.23, s32[]{:T(128)} %select_n.30), calls=%async_computation.15 | async-start | bytes 16896 | tf_op jit(solution)/shard_map/dynamic_slice | solution.py:187
  686.7 166.7 %all-to-all-start.3 = ((bf16[8,2,4096]{2,1,0:T(2,128)(2,1)}), bf16[8,2,4096]{2,1,0:T(2,128)(2,1)S(1)}, u32[]{:S(2)}, u32[]{:S(2)}) async-start(bf16[8,2,4096]{2,1,0:T(2,128)(2,1)} %reshape.108), calls=%async_computation.3 | async-start | bytes 262144 | tf_op jit(solution)/shard_map/all_to_all | solution.py:184
  940.9 14.9 %copy-start.1 = (bf16[8192,32]{0,1:T(8,128)(2,1)S(1)}, bf16[8192,32]{0,1:T(8,128)(2,1)}, u32[]{:S(2)}) copy-start(bf16[8192,32]{0,1:T(8,128)(2,1)} %param.24) | copy-start | bytes 1572868
Sparse Core Ops, SparseCore 0:
  10.6 42.5 all-gather.4
  55.4 17.2 all-gather.8
  74.3 56.9 all-gather.6
  133.3 57.1 all-gather.10
  344.4 125.4 reduce-scatter.7
  472.4 71.3 reduce-scatter.3
  574.6 277.0 all-reduce.8
  855.2 70.1 reduce-scatter.5
